TPU v7x, 32 devices: a whole 2x2x4 slice. The times are simulated.
32 devices in a mesh: gx: 4 (over z), gy: 4 (over y, x), gz: 2 (over core).
Axes of the slice: x: 2, y: 2, z: 4, core: 2. Of those that a mesh axis runs over, the one named last changes fastest.
Arguments:
- adjoint_residual: float32 [32, 64, 256], P('gx', 'gy', 'gz'), may hold values from -6 to 6
- face_x: float32 [32, 64, 256], P('gx', 'gy', 'gz'), may hold values from 0.03 to 30
- face_y: float32 [32, 64, 256], P('gx', 'gy', 'gz'), may hold values from 0.03 to 30
- face_z: float32 [32, 64, 256], P('gx', 'gy', 'gz'), may hold values from 0.03 to 30
Outputs:
- correction: float32 [32, 64, 256], P('gx', 'gy', 'gz')
All inputs are finite; a program needn't handle non-finite values.
Results may differ from a plain program's by a relative error of at most 0.0001.
Values sent between devices are 32-bit elements; how exact they have to be, the bound alone decides.
No kernel may reach another device: no remote copies, remote signals or barrier semaphores. Data moves between devices by JAX's collectives and lax.ppermute only.
A program may use at most 64 MiB of HBM per device.

v0:
```python
import jax
import jax.numpy as jnp
from jax import lax
from jax.sharding import PartitionSpec as P

LEVELS = 4
COARSE_ITERS = 6
damping = 2.0 / 3.0


def extended(block, sides, width):
    for axis, dim in sides:
        count = lax.axis_size(axis)
        forward = [(i, i + 1) for i in range(count - 1)]
        backward = [(target, source) for source, target in forward]
        low = lax.ppermute(
            lax.slice_in_dim(block, block.shape[dim] - width, None, axis=dim), axis, forward
        )
        high = lax.ppermute(lax.slice_in_dim(block, 0, width, axis=dim), axis, backward)
        block = jnp.concatenate([low, block, high], axis=dim)
    return block


def from_behind(block, axis, distance):
    devices = range(lax.axis_size(axis))
    route = [(i - distance, i) for i in devices if i - distance in devices]
    return lax.ppermute(block, axis, route)


def stencil(padded, field, coefs):
    low_x, high_x, low_y, high_y, low_z, high_z = coefs
    diagonal = low_x + high_x + low_y + high_y + low_z + high_z
    result = diagonal * field - low_x * padded[:-2, 1:-1, 1:-1] - high_x * padded[2:, 1:-1, 1:-1]
    result = result - low_y * padded[1:-1, :-2, 1:-1] - high_y * padded[1:-1, 2:, 1:-1]
    return result - low_z * padded[1:-1, 1:-1, :-2] - high_z * padded[1:-1, 1:-1, 2:]


def operate(field, coefs):
    padded = extended(field, (("gx", 0), ("gy", 1), ("gz", 2)), 1)
    return stencil(padded, field, coefs)


def operate_whole(field, coefs):
    return stencil(jnp.pad(field, 1), field, coefs)


def blocked(values):
    return values.reshape(values.shape[0] // 2, 2, values.shape[1] // 2, 2, values.shape[2] // 2, 2)


def coarse_face(values, dim, parity):
    others = tuple((2 * k + 1 for k in range(3) if k != dim))
    summed = jnp.sum(blocked(values), axis=others)
    return 0.5 * lax.index_in_dim(summed, parity, dim + 1, keepdims=False)


def coarsen(coefs):
    result = []
    for dim in range(3):
        result.append(coarse_face(coefs[2 * dim], dim, 0))
        result.append(coarse_face(coefs[2 * dim + 1], dim, 1))
    return tuple(result)


def restrict(values):
    return jnp.sum(blocked(values), axis=(1, 3, 5))


def prolong(values):
    shape_out = (values.shape[0] * 2, values.shape[1] * 2, values.shape[2] * 2)
    wide = jnp.broadcast_to(
        values[:, None, :, None, :, None],
        (values.shape[0], 2, values.shape[1], 2, values.shape[2], 2),
    )
    return wide.reshape(shape_out)


def total_local(value):
    return value


def conj_grad(rhs, coefs, apply_op, total):
    solution = jnp.zeros_like(rhs)
    remain = rhs
    search = rhs
    norm_now = total(jnp.sum(remain * remain))
    for step in range(COARSE_ITERS):
        image = apply_op(search, coefs)
        alpha = norm_now / total(jnp.sum(search * image))
        solution = solution + alpha * search
        remain = remain - alpha * image
        norm_next = total(jnp.sum(remain * remain))
        search = remain + norm_next / norm_now * search
        norm_now = norm_next
    return solution


def coarse_solve(rhs, coefs):
    part_x, part_y, part_z = rhs.shape
    count_x = lax.axis_size("gx")
    count_y = lax.axis_size("gy")
    count_z = lax.axis_size("gz")
    stacked = jnp.stack((rhs,) + coefs)[None]
    whole = lax.all_gather(stacked, ("gx", "gy", "gz"), axis=0, tiled=True)
    whole = whole.reshape(count_x, count_y, count_z, 7, part_x, part_y, part_z)
    whole = whole.transpose(3, 0, 4, 1, 5, 2, 6).reshape(
        7, count_x * part_x, count_y * part_y, count_z * part_z
    )
    whole_coefs = tuple((whole[k] for k in range(1, 7)))
    solution = conj_grad(whole[0], whole_coefs, operate_whole, total_local)
    starts = (
        lax.axis_index("gx") * part_x,
        lax.axis_index("gy") * part_y,
        lax.axis_index("gz") * part_z,
    )
    return lax.dynamic_slice(solution, starts, (part_x, part_y, part_z))


def cycle(rhs, levels_left, coefs):
    if levels_left == 1:
        return coarse_solve(rhs, coefs)
    diagonal = coefs[0] + coefs[1] + coefs[2] + coefs[3] + coefs[4] + coefs[5]
    field = damping * rhs / diagonal
    field = field + damping * (rhs - operate(field, coefs)) / diagonal
    remain = rhs - operate(field, coefs)
    field = field + prolong(cycle(restrict(remain), levels_left - 1, coarsen(coefs)))
    field = field + damping * (rhs - operate(field, coefs)) / diagonal
    return field


def per_device(adjoint_residual, face_x, face_y, face_z):
    rim_x = from_behind(face_x[:1], "gx", -1)
    rim_y = from_behind(face_y[:, :1], "gy", -1)
    rim_z = from_behind(face_z[:, :, :1], "gz", -1)
    high_x = jnp.concatenate([face_x[1:], rim_x], 0)
    high_y = jnp.concatenate([face_y[:, 1:], rim_y], 1)
    high_z = jnp.concatenate([face_z[:, :, 1:], rim_z], 2)
    coefs = (face_x, high_x, face_y, high_y, face_z, high_z)
    return cycle(adjoint_residual, LEVELS, coefs)


def solution(mesh):
    return jax.shard_map(
        per_device,
        mesh=mesh,
        in_specs=(
            P("gx", "gy", "gz"),
            P("gx", "gy", "gz"),
            P("gx", "gy", "gz"),
            P("gx", "gy", "gz"),
        ),
        out_specs=P("gx", "gy", "gz"),
        check_vma=False,
    )
```

profile of v0, /device:TPU:0, one launch (start us, length us, event | category | flops | bytes accessed | tf_op | source)
XLA Modules:
  0.0 335.5 jit_solution(15201036902934139529)
XLA Ops:
  5.4 6.3 %reshape.224 = f32[4,2,8,2,64,2]{5,4,3,2,1,0:T(8,128)} reshape(f32[8,16,128]{2,1,0:T(8,128)} %param.7) | data formatting | bytes 131072 | tf_op jit(solution)/shard_map/reshape | solution.py:48
  11.7 5.5 %reshape.222 = f32[4,2,8,2,64,2]{5,4,3,2,1,0:T(8,128)} reshape(f32[8,16,128]{2,1,0:T(8,128)S(1)} %copy-done) | data formatting | bytes 131072 | tf_op jit(solution)/shard_map/reshape | solution.py:48
  23.3 5.5 %reshape.220 = f32[4,2,8,2,64,2]{5,4,3,2,1,0:T(8,128)} reshape(f32[8,16,128]{2,1,0:T(8,128)S(1)} %copy-done.2) | data formatting | bytes 131072 | tf_op jit(solution)/shard_map/reshape | solution.py:48
  31.8 5.6 %collective-permute-start.3 = (f32[1,16,128]{2,1,0:T(8,128)S(1)}, f32[1,16,128]{2,1,0:T(8,128)S(1)}, u32[]{:S(2)}, u32[]{:S(2)}) collective-permute-start(f32[1,16,128]{2,1,0:T(8,128)S(1)} %get-tuple-element.49), channel_id=1, source_target_pairs={{0,8},{8,16},{16,24},{1,9},{9,17},{17,25},{2,10},{10,18},{18,26},{... | collective-permute-start | bytes 24584 | tf_op jit(solution)/shard_map/ppermute | solution.py:16
  39.4 3.5 %collective-permute-done.4 = f32[1,16,128]{2,1,0:T(8,128)S(1)} collective-permute-done((f32[1,16,128]{2,1,0:T(8,128)S(1)}, f32[1,16,128]{2,1,0:T(8,128)S(1)}, u32[]{:S(2)}, u32[]{:S(2)}) %collective-permute-start.4) | collective-permute-done | bytes 8224 | tf_op jit(solution)/shard_map/ppermute | solution.py:19
  43.0 4.5 %collective-permute-start.5 = (f32[10,1,128]{2,1,0:T(1,128)S(1)}, f32[10,1,128]{2,1,0:T(1,128)S(1)}, u32[]{:S(2)}, u32[]{:S(2)}) collective-permute-start(f32[10,1,128]{2,1,0:T(1,128)S(1)} %get-tuple-element.42), channel_id=1, source_target_pairs={{0,2},{2,4},{4,6},{1,3},{3,5},{5,7},{8,10},{10,12},{12,14},{9,11},... | collective-permute-start | bytes 15368 | tf_op jit(solution)/shard_map/ppermute | solution.py:16
  49.5 4.3 %collective-permute-done.6 = f32[10,1,128]{2,1,0:T(1,128)S(1)} collective-permute-done((f32[10,1,128]{2,1,0:T(1,128)S(1)}, f32[10,1,128]{2,1,0:T(1,128)S(1)}, u32[]{:S(2)}, u32[]{:S(2)}) %collective-permute-start.6) | collective-permute-done | bytes 5152 | tf_op jit(solution)/shard_map/ppermute | solution.py:19
  60.0 4.5 %collective-permute-start.9 = (f32[1,16,128]{2,1,0:T(8,128)S(1)}, f32[1,16,128]{2,1,0:T(8,128)S(1)}, u32[]{:S(2)}, u32[]{:S(2)}) collective-permute-start(f32[1,16,128]{2,1,0:T(8,128)S(1)} %get-tuple-element.47), channel_id=1, source_target_pairs={{0,8},{8,16},{16,24},{1,9},{9,17},{17,25},{2,10},{10,18},{18,26},{... | collective-permute-start | bytes 24584 | tf_op jit(solution)/shard_map/ppermute | solution.py:16
  65.9 4.8 %collective-permute-start.11 = (f32[10,1,128]{2,1,0:T(1,128)S(1)}, f32[10,1,128]{2,1,0:T(1,128)S(1)}, u32[]{:S(2)}, u32[]{:S(2)}) collective-permute-start(f32[10,1,128]{2,1,0:T(1,128)S(1)} %get-tuple-element.40), channel_id=1, source_target_pairs={{0,2},{2,4},{4,6},{1,3},{3,5},{5,7},{8,10},{10,12},{12,14},{9,11},... | collective-permute-start | bytes 15368 | tf_op jit(solution)/shard_map/ppermute | solution.py:16
  72.0 4.2 %collective-permute-done.12 = f32[10,1,128]{2,1,0:T(1,128)S(1)} collective-permute-done((f32[10,1,128]{2,1,0:T(1,128)S(1)}, f32[10,1,128]{2,1,0:T(1,128)S(1)}, u32[]{:S(2)}, u32[]{:S(2)}) %collective-permute-start.12) | collective-permute-done | bytes 5152 | tf_op jit(solution)/shard_map/ppermute | solution.py:19
  79.3 5.5 %reshape.225 = f32[4,2,8,2,64,2]{5,4,3,2,1,0:T(8,128)} reshape(f32[8,16,128]{2,1,0:T(8,128)S(1)} %get-tuple-element.23) | data formatting | bytes 131072 | tf_op jit(solution)/shard_map/reshape | solution.py:48
  84.8 5.5 %reshape.223 = f32[4,2,8,2,64,2]{5,4,3,2,1,0:T(8,128)} reshape(f32[8,16,128]{2,1,0:T(8,128)S(1)} %get-tuple-element.22) | data formatting | bytes 131072 | tf_op jit(solution)/shard_map/reshape | solution.py:48
  96.7 5.5 %reshape.221 = f32[4,2,8,2,64,2]{5,4,3,2,1,0:T(8,128)} reshape(f32[8,16,128]{2,1,0:T(8,128)S(1)} %get-tuple-element.46) | data formatting | bytes 131072 | tf_op jit(solution)/shard_map/reshape | solution.py:48
  105.2 5.5 %reshape.219 = f32[4,2,8,2,64,2]{5,4,3,2,1,0:T(8,128)} reshape(f32[8,16,128]{2,1,0:T(8,128)S(1)} %fusion.18) | data formatting | bytes 131072 | tf_op jit(solution)/shard_map/reshape | solution.py:48
  113.3 4.2 %collective-permute-start.15 = (f32[1,8,64]{2,1,0:T(8,128)S(1)}, f32[1,8,64]{2,1,0:T(8,128)S(1)}, u32[]{:S(2)}, u32[]{:S(2)}) collective-permute-start(f32[1,8,64]{2,1,0:T(8,128)S(1)} %get-tuple-element.73), channel_id=1, source_target_pairs={{0,8},{8,16},{16,24},{1,9},{9,17},{17,25},{2,10},{10,18},{18,26},{... | collective-permute-start | bytes 6152 | tf_op jit(solution)/shard_map/ppermute | solution.py:16
  119.0 4.0 %collective-permute-done.16 = f32[1,8,64]{2,1,0:T(8,128)S(1)} collective-permute-done((f32[1,8,64]{2,1,0:T(8,128)S(1)}, f32[1,8,64]{2,1,0:T(8,128)S(1)}, u32[]{:S(2)}, u32[]{:S(2)}) %collective-permute-start.16) | collective-permute-done | bytes 2080 | tf_op jit(solution)/shard_map/ppermute | solution.py:19
  127.1 4.2 %collective-permute-done.18 = f32[6,1,64]{2,1,0:T(1,128)S(1)} collective-permute-done((f32[6,1,64]{2,1,0:T(1,128)S(1)}, f32[6,1,64]{2,1,0:T(1,128)S(1)}, u32[]{:S(2)}, u32[]{:S(2)}) %collective-permute-start.18) | collective-permute-done | bytes 1568 | tf_op jit(solution)/shard_map/ppermute | solution.py:19
  135.9 3.5 %collective-permute-start.21 = (f32[1,8,64]{2,1,0:T(8,128)S(1)}, f32[1,8,64]{2,1,0:T(8,128)S(1)}, u32[]{:S(2)}, u32[]{:S(2)}) collective-permute-start(f32[1,8,64]{2,1,0:T(8,128)S(1)} %get-tuple-element.71), channel_id=1, source_target_pairs={{0,8},{8,16},{16,24},{1,9},{9,17},{17,25},{2,10},{10,18},{18,26},{... | collective-permute-start | bytes 6152 | tf_op jit(solution)/shard_map/ppermute | solution.py:16
  163.5 4.0 %collective-permute-done.28 = f32[1,4,32]{2,1,0:T(4,128)S(1)} collective-permute-done((f32[1,4,32]{2,1,0:T(4,128)S(1)}, f32[1,4,32]{2,1,0:T(4,128)S(1)}, u32[]{:S(2)}, u32[]{:S(2)}) %collective-permute-start.28) | collective-permute-done | bytes 544 | tf_op jit(solution)/shard_map/ppermute | solution.py:19
  171.7 4.2 %collective-permute-done.30 = f32[4,1,32]{2,1,0:T(1,128)S(1)} collective-permute-done((f32[4,1,32]{2,1,0:T(1,128)S(1)}, f32[4,1,32]{2,1,0:T(1,128)S(1)}, u32[]{:S(2)}, u32[]{:S(2)}) %collective-permute-start.30) | collective-permute-done | bytes 544 | tf_op jit(solution)/shard_map/ppermute | solution.py:19
  183.8 4.0 %collective-permute-done.34 = f32[1,4,32]{2,1,0:T(4,128)S(1)} collective-permute-done((f32[1,4,32]{2,1,0:T(4,128)S(1)}, f32[1,4,32]{2,1,0:T(4,128)S(1)}, u32[]{:S(2)}, u32[]{:S(2)}) %collective-permute-start.34) | collective-permute-done | bytes 544 | tf_op jit(solution)/shard_map/ppermute | solution.py:19
  192.1 4.0 %collective-permute-done.36 = f32[4,1,32]{2,1,0:T(1,128)S(1)} collective-permute-done((f32[4,1,32]{2,1,0:T(1,128)S(1)}, f32[4,1,32]{2,1,0:T(1,128)S(1)}, u32[]{:S(2)}, u32[]{:S(2)}) %collective-permute-start.36) | collective-permute-done | bytes 544 | tf_op jit(solution)/shard_map/ppermute | solution.py:19
  200.9 38.1 %all-gather = f32[224,1,2,16]{3,2,1,0:T(2,128)S(1)} all-gather(f32[7,1,2,16]{3,2,1,0:T(2,128)S(1)} %constant_dynamic-update-slice_fusion), channel_id=2, replica_groups=mesh['gx'=4,'gy'=4,'gz'=2] {'gx','gy','gz'}, dimensions={0}, use_global_device_ids=true | all-gather | bytes 29568 | tf_op jit(solution)/shard_map/all_gather | solution.py:104
  266.2 4.2 %collective-permute-done.40 = f32[1,4,32]{2,1,0:T(4,128)S(1)} collective-permute-done((f32[1,4,32]{2,1,0:T(4,128)S(1)}, f32[1,4,32]{2,1,0:T(4,128)S(1)}, u32[]{:S(2)}, u32[]{:S(2)}) %collective-permute-start.40) | collective-permute-done | bytes 544 | tf_op jit(solution)/shard_map/ppermute | solution.py:19
  274.7 4.2 %collective-permute-done.42 = f32[4,1,32]{2,1,0:T(1,128)S(1)} collective-permute-done((f32[4,1,32]{2,1,0:T(1,128)S(1)}, f32[4,1,32]{2,1,0:T(1,128)S(1)}, u32[]{:S(2)}, u32[]{:S(2)}) %collective-permute-start.42) | collective-permute-done | bytes 544 | tf_op jit(solution)/shard_map/ppermute | solution.py:19
  286.8 4.2 %collective-permute-done.46 = f32[1,8,64]{2,1,0:T(8,128)S(1)} collective-permute-done((f32[1,8,64]{2,1,0:T(8,128)S(1)}, f32[1,8,64]{2,1,0:T(8,128)S(1)}, u32[]{:S(2)}, u32[]{:S(2)}) %collective-permute-start.46) | collective-permute-done | bytes 2080 | tf_op jit(solution)/shard_map/ppermute | solution.py:19
  295.2 4.2 %collective-permute-done.48 = f32[6,1,64]{2,1,0:T(1,128)S(1)} collective-permute-done((f32[6,1,64]{2,1,0:T(1,128)S(1)}, f32[6,1,64]{2,1,0:T(1,128)S(1)}, u32[]{:S(2)}, u32[]{:S(2)}) %collective-permute-start.48) | collective-permute-done | bytes 1568 | tf_op jit(solution)/shard_map/ppermute | solution.py:19
  306.5 4.0 %reshape.229 = f32[8,16,128]{2,1,0:T(8,128)S(1)} reshape(f32[4,2,8,2,64,2]{5,4,3,2,1,0:T(8,128)} %broadcast_in_dim.33) | data formatting | bytes 131072 | tf_op jit(solution)/shard_map/reshape | solution.py:75
  310.5 3.9 %collective-permute-start.51 = (f32[1,16,128]{2,1,0:T(8,128)S(1)}, f32[1,16,128]{2,1,0:T(8,128)S(1)}, u32[]{:S(2)}, u32[]{:S(2)}) collective-permute-start(f32[1,16,128]{2,1,0:T(8,128)S(1)} %get-tuple-element.44), channel_id=1, source_target_pairs={{0,8},{8,16},{16,24},{1,9},{9,17},{17,25},{2,10},{10,18},{18,26},{... | collective-permute-start | bytes 24584 | tf_op jit(solution)/shard_map/ppermute | solution.py:16
  315.7 4.2 %collective-permute-done.52 = f32[1,16,128]{2,1,0:T(8,128)S(1)} collective-permute-done((f32[1,16,128]{2,1,0:T(8,128)S(1)}, f32[1,16,128]{2,1,0:T(8,128)S(1)}, u32[]{:S(2)}, u32[]{:S(2)}) %collective-permute-start.52) | collective-permute-done | bytes 8224 | tf_op jit(solution)/shard_map/ppermute | solution.py:19
  320.0 4.5 %collective-permute-start.53 = (f32[10,1,128]{2,1,0:T(1,128)S(1)}, f32[10,1,128]{2,1,0:T(1,128)S(1)}, u32[]{:S(2)}, u32[]{:S(2)}) collective-permute-start(f32[10,1,128]{2,1,0:T(1,128)S(1)} %get-tuple-element.38), channel_id=1, source_target_pairs={{0,2},{2,4},{4,6},{1,3},{3,5},{5,7},{8,10},{10,12},{12,14},{9,11},... | collective-permute-start | bytes 15368 | tf_op jit(solution)/shard_map/ppermute | solution.py:16
  325.8 4.2 %collective-permute-done.54 = f32[10,1,128]{2,1,0:T(1,128)S(1)} collective-permute-done((f32[10,1,128]{2,1,0:T(1,128)S(1)}, f32[10,1,128]{2,1,0:T(1,128)S(1)}, u32[]{:S(2)}, u32[]{:S(2)}) %collective-permute-start.54) | collective-permute-done | bytes 5152 | tf_op jit(solution)/shard_map/ppermute | solution.py:19
  (263 shorter events, 140.6 us)
Async XLA Ops:
  0.7 30.9 %collective-permute-start = (f32[1,16,128]{2,1,0:T(8,128)S(1)}, f32[1,16,128]{2,1,0:T(8,128)S(1)}, u32[]{:S(2)}, u32[]{:S(2)}) collective-permute-start(f32[1,16,128]{2,1,0:T(8,128)S(1)} %slice.587), channel_id=1, source_target_pairs={{8,0},{16,8},{24,16},{9,1},{17,9},{25,17},{10,2},{18,10},{26,18},{... | collective-permute-start | bytes 24584 | tf_op jit(solution)/shard_map/ppermute | solution.py:27
  2.0 29.6 %collective-permute-start.2 = (f32[8,16,1]{2,1,0:T(8,128)}, f32[8,16,1]{2,1,0:T(8,128)S(1)}, u32[]{:S(2)}, u32[]{:S(2)}) collective-permute-start(f32[8,16,1]{2,1,0:T(8,128)} %bitcast.288), channel_id=1, source_target_pairs={{1,0},{3,2},{5,4},{7,6},{9,8},{11,10},{13,12},{15,14},{17,16},{19,... | collective-permute-start | bytes 1544 | tf_op jit(solution)/shard_map/ppermute | solution.py:27
  4.1 27.6 %collective-permute-start.1 = (f32[8,1,128]{2,1,0:T(1,128)S(1)}, f32[8,1,128]{2,1,0:T(1,128)S(1)}, u32[]{:S(2)}, u32[]{:S(2)}) collective-permute-start(f32[8,1,128]{2,1,0:T(1,128)S(1)} %slice.589), channel_id=1, source_target_pairs={{2,0},{4,2},{6,4},{3,1},{5,3},{7,5},{10,8},{12,10},{14,12},{11,9},... | collective-permute-start | bytes 12296 | tf_op jit(solution)/shard_map/ppermute | solution.py:27
  31.8 7.6 %collective-permute-start.3 = (f32[1,16,128]{2,1,0:T(8,128)S(1)}, f32[1,16,128]{2,1,0:T(8,128)S(1)}, u32[]{:S(2)}, u32[]{:S(2)}) collective-permute-start(f32[1,16,128]{2,1,0:T(8,128)S(1)} %get-tuple-element.49), channel_id=1, source_target_pairs={{0,8},{8,16},{16,24},{1,9},{9,17},{17,25},{2,10},{10,18},{18,26},{... | collective-permute-start | bytes 24584 | tf_op jit(solution)/shard_map/ppermute | solution.py:16
  37.4 5.5 %collective-permute-start.4 = (f32[1,16,128]{2,1,0:T(8,128)S(1)}, f32[1,16,128]{2,1,0:T(8,128)S(1)}, u32[]{:S(2)}, u32[]{:S(2)}) collective-permute-start(f32[1,16,128]{2,1,0:T(8,128)S(1)} %get-tuple-element.50), channel_id=1, source_target_pairs={{8,0},{16,8},{24,16},{9,1},{17,9},{25,17},{10,2},{18,10},{26,18},{... | collective-permute-start | bytes 24584 | tf_op jit(solution)/shard_map/ppermute | solution.py:19
  43.0 6.6 %collective-permute-start.5 = (f32[10,1,128]{2,1,0:T(1,128)S(1)}, f32[10,1,128]{2,1,0:T(1,128)S(1)}, u32[]{:S(2)}, u32[]{:S(2)}) collective-permute-start(f32[10,1,128]{2,1,0:T(1,128)S(1)} %get-tuple-element.42), channel_id=1, source_target_pairs={{0,2},{2,4},{4,6},{1,3},{3,5},{5,7},{8,10},{10,12},{12,14},{9,11},... | collective-permute-start | bytes 15368 | tf_op jit(solution)/shard_map/ppermute | solution.py:16
  47.5 6.3 %collective-permute-start.6 = (f32[10,1,128]{2,1,0:T(1,128)S(1)}, f32[10,1,128]{2,1,0:T(1,128)S(1)}, u32[]{:S(2)}, u32[]{:S(2)}) collective-permute-start(f32[10,1,128]{2,1,0:T(1,128)S(1)} %get-tuple-element.43), channel_id=1, source_target_pairs={{2,0},{4,2},{6,4},{3,1},{5,3},{7,5},{10,8},{12,10},{14,12},{11,9},... | collective-permute-start | bytes 15368 | tf_op jit(solution)/shard_map/ppermute | solution.py:19
  58.7 6.6 %collective-permute-start.10 = (f32[1,16,128]{2,1,0:T(8,128)S(1)}, f32[1,16,128]{2,1,0:T(8,128)S(1)}, u32[]{:S(2)}, u32[]{:S(2)}) collective-permute-start(f32[1,16,128]{2,1,0:T(8,128)S(1)} %get-tuple-element.48), channel_id=1, source_target_pairs={{8,0},{16,8},{24,16},{9,1},{17,9},{25,17},{10,2},{18,10},{26,18},{... | collective-permute-start | bytes 24584 | tf_op jit(solution)/shard_map/ppermute | solution.py:19
  60.0 5.9 %collective-permute-start.9 = (f32[1,16,128]{2,1,0:T(8,128)S(1)}, f32[1,16,128]{2,1,0:T(8,128)S(1)}, u32[]{:S(2)}, u32[]{:S(2)}) collective-permute-start(f32[1,16,128]{2,1,0:T(8,128)S(1)} %get-tuple-element.47), channel_id=1, source_target_pairs={{0,8},{8,16},{16,24},{1,9},{9,17},{17,25},{2,10},{10,18},{18,26},{... | collective-permute-start | bytes 24584 | tf_op jit(solution)/shard_map/ppermute | solution.py:16
  65.9 6.1 %collective-permute-start.11 = (f32[10,1,128]{2,1,0:T(1,128)S(1)}, f32[10,1,128]{2,1,0:T(1,128)S(1)}, u32[]{:S(2)}, u32[]{:S(2)}) collective-permute-start(f32[10,1,128]{2,1,0:T(1,128)S(1)} %get-tuple-element.40), channel_id=1, source_target_pairs={{0,2},{2,4},{4,6},{1,3},{3,5},{5,7},{8,10},{10,12},{12,14},{9,11},... | collective-permute-start | bytes 15368 | tf_op jit(solution)/shard_map/ppermute | solution.py:16
  70.7 5.5 %collective-permute-start.12 = (f32[10,1,128]{2,1,0:T(1,128)S(1)}, f32[10,1,128]{2,1,0:T(1,128)S(1)}, u32[]{:S(2)}, u32[]{:S(2)}) collective-permute-start(f32[10,1,128]{2,1,0:T(1,128)S(1)} %get-tuple-element.41), channel_id=1, source_target_pairs={{2,0},{4,2},{6,4},{3,1},{5,3},{7,5},{10,8},{12,10},{14,12},{11,9},... | collective-permute-start | bytes 15368 | tf_op jit(solution)/shard_map/ppermute | solution.py:19
  76.3 28.7 %collective-permute-start.13 = (f32[10,18,1]{2,1,0:T(8,128)S(1)}, f32[10,18,1]{2,1,0:T(8,128)S(1)}, u32[]{:S(2)}, u32[]{:S(2)}) collective-permute-start(f32[10,18,1]{2,1,0:T(8,128)S(1)} %get-tuple-element.34), channel_id=1, source_target_pairs={{0,1},{2,3},{4,5},{6,7},{8,9},{10,11},{12,13},{14,15},{16,17},{18,... | collective-permute-start | bytes 2168 | tf_op jit(solution)/shard_map/ppermute | solution.py:16
  77.6 27.4 %collective-permute-start.14 = (f32[10,18,1]{2,1,0:T(8,128)S(1)}, f32[10,18,1]{2,1,0:T(8,128)S(1)}, u32[]{:S(2)}, u32[]{:S(2)}) collective-permute-start(f32[10,18,1]{2,1,0:T(8,128)S(1)} %get-tuple-element.35), channel_id=1, source_target_pairs={{1,0},{3,2},{5,4},{7,6},{9,8},{11,10},{13,12},{15,14},{17,16},{19,... | collective-permute-start | bytes 2168 | tf_op jit(solution)/shard_map/ppermute | solution.py:19
  113.3 5.7 %collective-permute-start.15 = (f32[1,8,64]{2,1,0:T(8,128)S(1)}, f32[1,8,64]{2,1,0:T(8,128)S(1)}, u32[]{:S(2)}, u32[]{:S(2)}) collective-permute-start(f32[1,8,64]{2,1,0:T(8,128)S(1)} %get-tuple-element.73), channel_id=1, source_target_pairs={{0,8},{8,16},{16,24},{1,9},{9,17},{17,25},{2,10},{10,18},{18,26},{... | collective-permute-start | bytes 6152 | tf_op jit(solution)/shard_map/ppermute | solution.py:16
  117.5 5.5 %collective-permute-start.16 = (f32[1,8,64]{2,1,0:T(8,128)S(1)}, f32[1,8,64]{2,1,0:T(8,128)S(1)}, u32[]{:S(2)}, u32[]{:S(2)}) collective-permute-start(f32[1,8,64]{2,1,0:T(8,128)S(1)} %get-tuple-element.74), channel_id=1, source_target_pairs={{8,0},{16,8},{24,16},{9,1},{17,9},{25,17},{10,2},{18,10},{26,18},{... | collective-permute-start | bytes 6152 | tf_op jit(solution)/shard_map/ppermute | solution.py:19
  125.8 5.5 %collective-permute-start.18 = (f32[6,1,64]{2,1,0:T(1,128)S(1)}, f32[6,1,64]{2,1,0:T(1,128)S(1)}, u32[]{:S(2)}, u32[]{:S(2)}) collective-permute-start(f32[6,1,64]{2,1,0:T(1,128)S(1)} %get-tuple-element.62), channel_id=1, source_target_pairs={{2,0},{4,2},{6,4},{3,1},{5,3},{7,5},{10,8},{12,10},{14,12},{11,9},... | collective-permute-start | bytes 4616 | tf_op jit(solution)/shard_map/ppermute | solution.py:19
  135.9 5.5 %collective-permute-start.21 = (f32[1,8,64]{2,1,0:T(8,128)S(1)}, f32[1,8,64]{2,1,0:T(8,128)S(1)}, u32[]{:S(2)}, u32[]{:S(2)}) collective-permute-start(f32[1,8,64]{2,1,0:T(8,128)S(1)} %get-tuple-element.71), channel_id=1, source_target_pairs={{0,8},{8,16},{16,24},{1,9},{9,17},{17,25},{2,10},{10,18},{18,26},{... | collective-permute-start | bytes 6152 | tf_op jit(solution)/shard_map/ppermute | solution.py:16
  139.4 5.5 %collective-permute-start.22 = (f32[1,8,64]{2,1,0:T(8,128)S(1)}, f32[1,8,64]{2,1,0:T(8,128)S(1)}, u32[]{:S(2)}, u32[]{:S(2)}) collective-permute-start(f32[1,8,64]{2,1,0:T(8,128)S(1)} %get-tuple-element.72), channel_id=1, source_target_pairs={{8,0},{16,8},{24,16},{9,1},{17,9},{25,17},{10,2},{18,10},{26,18},{... | collective-permute-start | bytes 6152 | tf_op jit(solution)/shard_map/ppermute | solution.py:19
  147.7 5.5 %collective-permute-start.24 = (f32[6,1,64]{2,1,0:T(1,128)S(1)}, f32[6,1,64]{2,1,0:T(1,128)S(1)}, u32[]{:S(2)}, u32[]{:S(2)}) collective-permute-start(f32[6,1,64]{2,1,0:T(1,128)S(1)} %get-tuple-element.60), channel_id=1, source_target_pairs={{2,0},{4,2},{6,4},{3,1},{5,3},{7,5},{10,8},{12,10},{14,12},{11,9},... | collective-permute-start | bytes 4616 | tf_op jit(solution)/shard_map/ppermute | solution.py:19
  158.5 5.0 %collective-permute-start.27 = (f32[1,4,32]{2,1,0:T(4,128)S(1)}, f32[1,4,32]{2,1,0:T(4,128)S(1)}, u32[]{:S(2)}, u32[]{:S(2)}) collective-permute-start(f32[1,4,32]{2,1,0:T(4,128)S(1)} %get-tuple-element.85), channel_id=1, source_target_pairs={{0,8},{8,16},{16,24},{1,9},{9,17},{17,25},{2,10},{10,18},{18,26},{... | collective-permute-start | bytes 1544 | tf_op jit(solution)/shard_map/ppermute | solution.py:16
  162.0 5.5 %collective-permute-start.28 = (f32[1,4,32]{2,1,0:T(4,128)S(1)}, f32[1,4,32]{2,1,0:T(4,128)S(1)}, u32[]{:S(2)}, u32[]{:S(2)}) collective-permute-start(f32[1,4,32]{2,1,0:T(4,128)S(1)} %get-tuple-element.86), channel_id=1, source_target_pairs={{8,0},{16,8},{24,16},{9,1},{17,9},{25,17},{10,2},{18,10},{26,18},{... | collective-permute-start | bytes 1544 | tf_op jit(solution)/shard_map/ppermute | solution.py:19
  170.3 5.5 %collective-permute-start.30 = (f32[4,1,32]{2,1,0:T(1,128)S(1)}, f32[4,1,32]{2,1,0:T(1,128)S(1)}, u32[]{:S(2)}, u32[]{:S(2)}) collective-permute-start(f32[4,1,32]{2,1,0:T(1,128)S(1)} %get-tuple-element.80), channel_id=1, source_target_pairs={{2,0},{4,2},{6,4},{3,1},{5,3},{7,5},{10,8},{12,10},{14,12},{11,9},... | collective-permute-start | bytes 1544 | tf_op jit(solution)/shard_map/ppermute | solution.py:19
  182.3 5.5 %collective-permute-start.34 = (f32[1,4,32]{2,1,0:T(4,128)S(1)}, f32[1,4,32]{2,1,0:T(4,128)S(1)}, u32[]{:S(2)}, u32[]{:S(2)}) collective-permute-start(f32[1,4,32]{2,1,0:T(4,128)S(1)} %get-tuple-element.84), channel_id=1, source_target_pairs={{8,0},{16,8},{24,16},{9,1},{17,9},{25,17},{10,2},{18,10},{26,18},{... | collective-permute-start | bytes 1544 | tf_op jit(solution)/shard_map/ppermute | solution.py:19
  190.6 5.5 %collective-permute-start.36 = (f32[4,1,32]{2,1,0:T(1,128)S(1)}, f32[4,1,32]{2,1,0:T(1,128)S(1)}, u32[]{:S(2)}, u32[]{:S(2)}) collective-permute-start(f32[4,1,32]{2,1,0:T(1,128)S(1)} %get-tuple-element.78), channel_id=1, source_target_pairs={{2,0},{4,2},{6,4},{3,1},{5,3},{7,5},{10,8},{12,10},{14,12},{11,9},... | collective-permute-start | bytes 1544 | tf_op jit(solution)/shard_map/ppermute | solution.py:19
  264.9 5.5 %collective-permute-start.40 = (f32[1,4,32]{2,1,0:T(4,128)S(1)}, f32[1,4,32]{2,1,0:T(4,128)S(1)}, u32[]{:S(2)}, u32[]{:S(2)}) collective-permute-start(f32[1,4,32]{2,1,0:T(4,128)S(1)} %get-tuple-element.82), channel_id=1, source_target_pairs={{8,0},{16,8},{24,16},{9,1},{17,9},{25,17},{10,2},{18,10},{26,18},{... | collective-permute-start | bytes 1544 | tf_op jit(solution)/shard_map/ppermute | solution.py:19
  273.4 5.5 %collective-permute-start.42 = (f32[4,1,32]{2,1,0:T(1,128)S(1)}, f32[4,1,32]{2,1,0:T(1,128)S(1)}, u32[]{:S(2)}, u32[]{:S(2)}) collective-permute-start(f32[4,1,32]{2,1,0:T(1,128)S(1)} %get-tuple-element.76), channel_id=1, source_target_pairs={{2,0},{4,2},{6,4},{3,1},{5,3},{7,5},{10,8},{12,10},{14,12},{11,9},... | collective-permute-start | bytes 1544 | tf_op jit(solution)/shard_map/ppermute | solution.py:19
  285.5 5.5 %collective-permute-start.46 = (f32[1,8,64]{2,1,0:T(8,128)S(1)}, f32[1,8,64]{2,1,0:T(8,128)S(1)}, u32[]{:S(2)}, u32[]{:S(2)}) collective-permute-start(f32[1,8,64]{2,1,0:T(8,128)S(1)} %get-tuple-element.64), channel_id=1, source_target_pairs={{8,0},{16,8},{24,16},{9,1},{17,9},{25,17},{10,2},{18,10},{26,18},{... | collective-permute-start | bytes 6152 | tf_op jit(solution)/shard_map/ppermute | solution.py:19
  293.9 5.5 %collective-permute-start.48 = (f32[6,1,64]{2,1,0:T(1,128)S(1)}, f32[6,1,64]{2,1,0:T(1,128)S(1)}, u32[]{:S(2)}, u32[]{:S(2)}) collective-permute-start(f32[6,1,64]{2,1,0:T(1,128)S(1)} %get-tuple-element.58), channel_id=1, source_target_pairs={{2,0},{4,2},{6,4},{3,1},{5,3},{7,5},{10,8},{12,10},{14,12},{11,9},... | collective-permute-start | bytes 4616 | tf_op jit(solution)/shard_map/ppermute | solution.py:19
  310.5 5.2 %collective-permute-start.51 = (f32[1,16,128]{2,1,0:T(8,128)S(1)}, f32[1,16,128]{2,1,0:T(8,128)S(1)}, u32[]{:S(2)}, u32[]{:S(2)}) collective-permute-start(f32[1,16,128]{2,1,0:T(8,128)S(1)} %get-tuple-element.44), channel_id=1, source_target_pairs={{0,8},{8,16},{16,24},{1,9},{9,17},{17,25},{2,10},{10,18},{18,26},{... | collective-permute-start | bytes 24584 | tf_op jit(solution)/shard_map/ppermute | solution.py:16
  314.4 5.5 %collective-permute-start.52 = (f32[1,16,128]{2,1,0:T(8,128)S(1)}, f32[1,16,128]{2,1,0:T(8,128)S(1)}, u32[]{:S(2)}, u32[]{:S(2)}) collective-permute-start(f32[1,16,128]{2,1,0:T(8,128)S(1)} %get-tuple-element.45), channel_id=1, source_target_pairs={{8,0},{16,8},{24,16},{9,1},{17,9},{25,17},{10,2},{18,10},{26,18},{... | collective-permute-start | bytes 24584 | tf_op jit(solution)/shard_map/ppermute | solution.py:19
  320.0 5.9 %collective-permute-start.53 = (f32[10,1,128]{2,1,0:T(1,128)S(1)}, f32[10,1,128]{2,1,0:T(1,128)S(1)}, u32[]{:S(2)}, u32[]{:S(2)}) collective-permute-start(f32[10,1,128]{2,1,0:T(1,128)S(1)} %get-tuple-element.38), channel_id=1, source_target_pairs={{0,2},{2,4},{4,6},{1,3},{3,5},{5,7},{8,10},{10,12},{12,14},{9,11},... | collective-permute-start | bytes 15368 | tf_op jit(solution)/shard_map/ppermute | solution.py:16
  324.5 5.5 %collective-permute-start.54 = (f32[10,1,128]{2,1,0:T(1,128)S(1)}, f32[10,1,128]{2,1,0:T(1,128)S(1)}, u32[]{:S(2)}, u32[]{:S(2)}) collective-permute-start(f32[10,1,128]{2,1,0:T(1,128)S(1)} %get-tuple-element.39), channel_id=1, source_target_pairs={{2,0},{4,2},{6,4},{3,1},{5,3},{7,5},{10,8},{12,10},{14,12},{11,9},... | collective-permute-start | bytes 15368 | tf_op jit(solution)/shard_map/ppermute | solution.py:19
  (29 other events, 113.9 us)
where the time goes:
time: 338 us; the launch traced here: 335 us
  starting transfers between devices  112 us (33%)
  waiting for transfers between devices  82.6 us (24%)
  local copies, waits for them, and re-layouts  55.4 us (16%)
  blocking collectives  38.1 us (11%)
  other arithmetic  31.3 us (9%)
  between operations  16.5 us (5%)
    ppermute x27, waiting for transfers between devices, extended(): lax.ppermute(lax.slice_in_dim(block, 0, width, axis=dim), axis, backward)  81.9 us
    ppermute x27, starting transfers between devices, extended(): lax.ppermute(lax.slice_in_dim(block, block.shape[dim] - width, None, axis...  72.6 us
    reshape x8, local copies, waits for them, and re-layouts, blocked(): values.reshape(values.shape[0] // 2, 2, values.shape[1] // 2, 2, values.s...  39.8 us
    all_gather x1, blocking collectives, coarse_solve(): whole = lax.all_gather(stacked, ('gx', 'gy', 'gz'), axis=0, tiled=True)  38.1 us
    ppermute x27, starting transfers between devices, extended(): lax.ppermute(lax.slice_in_dim(block, 0, width, axis=dim), axis, backward)  35.1 us
    reduce_sum x22, other arithmetic, coarse_face(): summed = jnp.sum(blocked(values), axis=others)  18 us
  transfers between devices with their start and end apart: 57, of which 26 were waited for; matrix products, arithmetic and copies ran while one was open for 17% of the time, Pallas kernels for 0%

commit v1 on v0

--- a/solution.py
+++ b/solution.py
@@ -101,7 +101,15 @@
     count_y = lax.axis_size("gy")
     count_z = lax.axis_size("gz")
     stacked = jnp.stack((rhs,) + coefs)[None]
-    whole = lax.all_gather(stacked, ("gx", "gy", "gz"), axis=0, tiled=True)
+    ways, here = (lax.axis_size(("gx", "gy", "gz")), lax.axis_index(("gx", "gy", "gz")))
+    grown, reach = (stacked, 1)
+    while reach < ways:
+        theirs = lax.ppermute(grown, ("gx", "gy", "gz"), [(d, d ^ reach) for d in range(ways)])
+        mine_first = jnp.concatenate([grown, theirs], axis=0)
+        theirs_first = jnp.concatenate([theirs, grown], axis=0)
+        grown = jnp.where(here & reach == 0, mine_first, theirs_first)
+        reach = 2 * reach
+    whole = grown
     whole = whole.reshape(count_x, count_y, count_z, 7, part_x, part_y, part_z)
     whole = whole.transpose(3, 0, 4, 1, 5, 2, 6).reshape(
         7, count_x * part_x, count_y * part_y, count_z * part_z

time: 338 us -> 317 us (0.938)
  blocking collectives: 38.1 us -> 0 us
  waiting for transfers between devices: 82.6 us -> 101 us
    all_gather x1 -> x0, blocking collectives: 38.1 us -> none  [coarse_solve(): whole = lax.all_gather(stacked, ('gx', 'gy', 'gz'), axis=0, tiled=True)]
    ppermute x0 -> x5, waiting for transfers between devices: none -> 18.4 us  [coarse_solve(): lax.ppermute(grown, ('gx', 'gy', 'gz'), [(d, d ^ reach) for d in range(wa...]
  transfers between devices with their start and end apart: 57 -> 62, of which waited for: 26 -> 31; matrix products, arithmetic and copies ran while one was open for 17% -> 18% of each run, Pallas kernels for 0% -> 0%
where the time goes in v1:
time: 317 us; the launch traced here: 315 us
  starting transfers between devices  111 us (35%)
  waiting for transfers between devices  101 us (32%)
  local copies, waits for them, and re-layouts  55.4 us (17%)
  other arithmetic  31.6 us (10%)
  between operations  16.6 us (5%)
    ppermute x27, waiting for transfers between devices, extended(): lax.ppermute(lax.slice_in_dim(block, 0, width, axis=dim), axis, backward)  81.6 us
    ppermute x27, starting transfers between devices, extended(): lax.ppermute(lax.slice_in_dim(block, block.shape[dim] - width, None, axis...  70 us
    reshape x8, local copies, waits for them, and re-layouts, blocked(): values.reshape(values.shape[0] // 2, 2, values.shape[1] // 2, 2, values.s...  39.8 us
    ppermute x27, starting transfers between devices, extended(): lax.ppermute(lax.slice_in_dim(block, 0, width, axis=dim), axis, backward)  35.3 us
    ppermute x5, waiting for transfers between devices, coarse_solve(): lax.ppermute(grown, ('gx', 'gy', 'gz'), [(d, d ^ reach) for d in range(wa...  18.4 us
    reduce_sum x22, other arithmetic, coarse_face(): summed = jnp.sum(blocked(values), axis=others)  18 us
  transfers between devices with their start and end apart: 62, of which 31 were waited for; matrix products, arithmetic and copies ran while one was open for 18% of the time, Pallas kernels for 0%

profile of v1, /device:TPU:0, one launch (start us, length us, event | category | flops | bytes accessed | tf_op | source)
XLA Modules:
  0.0 315.1 jit_solution(1506109364347475774)
XLA Ops:
  5.4 6.3 %reshape.692 = f32[4,2,8,2,64,2]{5,4,3,2,1,0:T(8,128)} reshape(f32[8,16,128]{2,1,0:T(8,128)} %param.7) | data formatting | bytes 131072 | tf_op jit(solution)/shard_map/reshape | solution.py:48
  11.7 5.5 %reshape.690 = f32[4,2,8,2,64,2]{5,4,3,2,1,0:T(8,128)} reshape(f32[8,16,128]{2,1,0:T(8,128)S(1)} %copy-done) | data formatting | bytes 131072 | tf_op jit(solution)/shard_map/reshape | solution.py:48
  23.3 5.5 %reshape.688 = f32[4,2,8,2,64,2]{5,4,3,2,1,0:T(8,128)} reshape(f32[8,16,128]{2,1,0:T(8,128)S(1)} %copy-done.2) | data formatting | bytes 131072 | tf_op jit(solution)/shard_map/reshape | solution.py:48
  31.8 5.6 %collective-permute-start.3 = (f32[1,16,128]{2,1,0:T(8,128)S(1)}, f32[1,16,128]{2,1,0:T(8,128)S(1)}, u32[]{:S(2)}, u32[]{:S(2)}) collective-permute-start(f32[1,16,128]{2,1,0:T(8,128)S(1)} %get-tuple-element.49), channel_id=1, source_target_pairs={{0,8},{8,16},{16,24},{1,9},{9,17},{17,25},{2,10},{10,18},{18,26},{... | collective-permute-start | bytes 24584 | tf_op jit(solution)/shard_map/ppermute | solution.py:16
  39.4 3.5 %collective-permute-done.4 = f32[1,16,128]{2,1,0:T(8,128)S(1)} collective-permute-done((f32[1,16,128]{2,1,0:T(8,128)S(1)}, f32[1,16,128]{2,1,0:T(8,128)S(1)}, u32[]{:S(2)}, u32[]{:S(2)}) %collective-permute-start.4) | collective-permute-done | bytes 8224 | tf_op jit(solution)/shard_map/ppermute | solution.py:19
  43.0 4.5 %collective-permute-start.5 = (f32[10,1,128]{2,1,0:T(1,128)S(1)}, f32[10,1,128]{2,1,0:T(1,128)S(1)}, u32[]{:S(2)}, u32[]{:S(2)}) collective-permute-start(f32[10,1,128]{2,1,0:T(1,128)S(1)} %get-tuple-element.42), channel_id=1, source_target_pairs={{0,2},{2,4},{4,6},{1,3},{3,5},{5,7},{8,10},{10,12},{12,14},{9,11},... | collective-permute-start | bytes 15368 | tf_op jit(solution)/shard_map/ppermute | solution.py:16
  49.5 4.3 %collective-permute-done.6 = f32[10,1,128]{2,1,0:T(1,128)S(1)} collective-permute-done((f32[10,1,128]{2,1,0:T(1,128)S(1)}, f32[10,1,128]{2,1,0:T(1,128)S(1)}, u32[]{:S(2)}, u32[]{:S(2)}) %collective-permute-start.6) | collective-permute-done | bytes 5152 | tf_op jit(solution)/shard_map/ppermute | solution.py:19
  60.0 4.5 %collective-permute-start.9 = (f32[1,16,128]{2,1,0:T(8,128)S(1)}, f32[1,16,128]{2,1,0:T(8,128)S(1)}, u32[]{:S(2)}, u32[]{:S(2)}) collective-permute-start(f32[1,16,128]{2,1,0:T(8,128)S(1)} %get-tuple-element.47), channel_id=1, source_target_pairs={{0,8},{8,16},{16,24},{1,9},{9,17},{17,25},{2,10},{10,18},{18,26},{... | collective-permute-start | bytes 24584 | tf_op jit(solution)/shard_map/ppermute | solution.py:16
  65.9 4.8 %collective-permute-start.11 = (f32[10,1,128]{2,1,0:T(1,128)S(1)}, f32[10,1,128]{2,1,0:T(1,128)S(1)}, u32[]{:S(2)}, u32[]{:S(2)}) collective-permute-start(f32[10,1,128]{2,1,0:T(1,128)S(1)} %get-tuple-element.40), channel_id=1, source_target_pairs={{0,2},{2,4},{4,6},{1,3},{3,5},{5,7},{8,10},{10,12},{12,14},{9,11},... | collective-permute-start | bytes 15368 | tf_op jit(solution)/shard_map/ppermute | solution.py:16
  72.0 4.2 %collective-permute-done.12 = f32[10,1,128]{2,1,0:T(1,128)S(1)} collective-permute-done((f32[10,1,128]{2,1,0:T(1,128)S(1)}, f32[10,1,128]{2,1,0:T(1,128)S(1)}, u32[]{:S(2)}, u32[]{:S(2)}) %collective-permute-start.12) | collective-permute-done | bytes 5152 | tf_op jit(solution)/shard_map/ppermute | solution.py:19
  79.3 5.5 %reshape.693 = f32[4,2,8,2,64,2]{5,4,3,2,1,0:T(8,128)} reshape(f32[8,16,128]{2,1,0:T(8,128)S(1)} %get-tuple-element.23) | data formatting | bytes 131072 | tf_op jit(solution)/shard_map/reshape | solution.py:48
  84.8 5.5 %reshape.691 = f32[4,2,8,2,64,2]{5,4,3,2,1,0:T(8,128)} reshape(f32[8,16,128]{2,1,0:T(8,128)S(1)} %get-tuple-element.22) | data formatting | bytes 131072 | tf_op jit(solution)/shard_map/reshape | solution.py:48
  96.7 5.5 %reshape.689 = f32[4,2,8,2,64,2]{5,4,3,2,1,0:T(8,128)} reshape(f32[8,16,128]{2,1,0:T(8,128)S(1)} %get-tuple-element.46) | data formatting | bytes 131072 | tf_op jit(solution)/shard_map/reshape | solution.py:48
  105.2 5.5 %reshape.687 = f32[4,2,8,2,64,2]{5,4,3,2,1,0:T(8,128)} reshape(f32[8,16,128]{2,1,0:T(8,128)S(1)} %fusion.18) | data formatting | bytes 131072 | tf_op jit(solution)/shard_map/reshape | solution.py:48
  113.3 4.2 %collective-permute-start.15 = (f32[1,8,64]{2,1,0:T(8,128)S(1)}, f32[1,8,64]{2,1,0:T(8,128)S(1)}, u32[]{:S(2)}, u32[]{:S(2)}) collective-permute-start(f32[1,8,64]{2,1,0:T(8,128)S(1)} %get-tuple-element.73), channel_id=1, source_target_pairs={{0,8},{8,16},{16,24},{1,9},{9,17},{17,25},{2,10},{10,18},{18,26},{... | collective-permute-start | bytes 6152 | tf_op jit(solution)/shard_map/ppermute | solution.py:16
  119.0 4.0 %collective-permute-done.16 = f32[1,8,64]{2,1,0:T(8,128)S(1)} collective-permute-done((f32[1,8,64]{2,1,0:T(8,128)S(1)}, f32[1,8,64]{2,1,0:T(8,128)S(1)}, u32[]{:S(2)}, u32[]{:S(2)}) %collective-permute-start.16) | collective-permute-done | bytes 2080 | tf_op jit(solution)/shard_map/ppermute | solution.py:19
  127.1 4.2 %collective-permute-done.18 = f32[6,1,64]{2,1,0:T(1,128)S(1)} collective-permute-done((f32[6,1,64]{2,1,0:T(1,128)S(1)}, f32[6,1,64]{2,1,0:T(1,128)S(1)}, u32[]{:S(2)}, u32[]{:S(2)}) %collective-permute-start.18) | collective-permute-done | bytes 1568 | tf_op jit(solution)/shard_map/ppermute | solution.py:19
  135.9 3.5 %collective-permute-start.21 = (f32[1,8,64]{2,1,0:T(8,128)S(1)}, f32[1,8,64]{2,1,0:T(8,128)S(1)}, u32[]{:S(2)}, u32[]{:S(2)}) collective-permute-start(f32[1,8,64]{2,1,0:T(8,128)S(1)} %get-tuple-element.71), channel_id=1, source_target_pairs={{0,8},{8,16},{16,24},{1,9},{9,17},{17,25},{2,10},{10,18},{18,26},{... | collective-permute-start | bytes 6152 | tf_op jit(solution)/shard_map/ppermute | solution.py:16
  163.5 4.0 %collective-permute-done.28 = f32[1,4,32]{2,1,0:T(4,128)S(1)} collective-permute-done((f32[1,4,32]{2,1,0:T(4,128)S(1)}, f32[1,4,32]{2,1,0:T(4,128)S(1)}, u32[]{:S(2)}, u32[]{:S(2)}) %collective-permute-start.28) | collective-permute-done | bytes 544 | tf_op jit(solution)/shard_map/ppermute | solution.py:19
  171.7 4.2 %collective-permute-done.30 = f32[4,1,32]{2,1,0:T(1,128)S(1)} collective-permute-done((f32[4,1,32]{2,1,0:T(1,128)S(1)}, f32[4,1,32]{2,1,0:T(1,128)S(1)}, u32[]{:S(2)}, u32[]{:S(2)}) %collective-permute-start.30) | collective-permute-done | bytes 544 | tf_op jit(solution)/shard_map/ppermute | solution.py:19
  183.8 4.0 %collective-permute-done.34 = f32[1,4,32]{2,1,0:T(4,128)S(1)} collective-permute-done((f32[1,4,32]{2,1,0:T(4,128)S(1)}, f32[1,4,32]{2,1,0:T(4,128)S(1)}, u32[]{:S(2)}, u32[]{:S(2)}) %collective-permute-start.34) | collective-permute-done | bytes 544 | tf_op jit(solution)/shard_map/ppermute | solution.py:19
  192.1 4.0 %collective-permute-done.36 = f32[4,1,32]{2,1,0:T(1,128)S(1)} collective-permute-done((f32[4,1,32]{2,1,0:T(1,128)S(1)}, f32[4,1,32]{2,1,0:T(1,128)S(1)}, u32[]{:S(2)}, u32[]{:S(2)}) %collective-permute-start.36) | collective-permute-done | bytes 544 | tf_op jit(solution)/shard_map/ppermute | solution.py:19
  206.1 3.8 %collective-permute-done.41 = f32[4,7,1,2,16]{4,3,1,2,0:T(2,128)S(1)} collective-permute-done((f32[4,7,1,2,16]{4,3,1,2,0:T(2,128)S(1)}, f32[4,7,1,2,16]{4,3,1,2,0:T(2,128)S(1)}, u32[]{:S(2)}, u32[]{:S(2)}) %collective-permute-start.41) | collective-permute-done | bytes 3616 | tf_op jit(solution)/shard_map/ppermute | solution.py:107
  210.1 4.1 %collective-permute-done.42 = f32[8,7,1,2,16]{4,3,1,2,0:T(2,128)S(1)} collective-permute-done((f32[8,7,1,2,16]{4,3,1,2,0:T(2,128)S(1)}, f32[8,7,1,2,16]{4,3,1,2,0:T(2,128)S(1)}, u32[]{:S(2)}, u32[]{:S(2)}) %collective-permute-start.42) | collective-permute-done | bytes 7200 | tf_op jit(solution)/shard_map/ppermute | solution.py:107
  214.4 6.6 %collective-permute-done.43 = f32[16,7,1,2,16]{4,3,1,2,0:T(2,128)S(1)} collective-permute-done((f32[16,7,1,2,16]{4,3,1,2,0:T(2,128)S(1)}, f32[16,7,1,2,16]{4,3,1,2,0:T(2,128)S(1)}, u32[]{:S(2)}, u32[]{:S(2)}) %collective-permute-start.43) | collective-permute-done | bytes 14368 | tf_op jit(solution)/shard_map/ppermute | solution.py:107
  248.5 4.2 %collective-permute-done.45 = f32[1,4,32]{2,1,0:T(4,128)S(1)} collective-permute-done((f32[1,4,32]{2,1,0:T(4,128)S(1)}, f32[1,4,32]{2,1,0:T(4,128)S(1)}, u32[]{:S(2)}, u32[]{:S(2)}) %collective-permute-start.45) | collective-permute-done | bytes 544 | tf_op jit(solution)/shard_map/ppermute | solution.py:19
  256.8 4.2 %collective-permute-done.47 = f32[4,1,32]{2,1,0:T(1,128)S(1)} collective-permute-done((f32[4,1,32]{2,1,0:T(1,128)S(1)}, f32[4,1,32]{2,1,0:T(1,128)S(1)}, u32[]{:S(2)}, u32[]{:S(2)}) %collective-permute-start.47) | collective-permute-done | bytes 544 | tf_op jit(solution)/shard_map/ppermute | solution.py:19
  269.8 4.2 %collective-permute-done.51 = f32[1,8,64]{2,1,0:T(8,128)S(1)} collective-permute-done((f32[1,8,64]{2,1,0:T(8,128)S(1)}, f32[1,8,64]{2,1,0:T(8,128)S(1)}, u32[]{:S(2)}, u32[]{:S(2)}) %collective-permute-start.51) | collective-permute-done | bytes 2080 | tf_op jit(solution)/shard_map/ppermute | solution.py:19
  278.4 4.2 %collective-permute-done.53 = f32[6,1,64]{2,1,0:T(1,128)S(1)} collective-permute-done((f32[6,1,64]{2,1,0:T(1,128)S(1)}, f32[6,1,64]{2,1,0:T(1,128)S(1)}, u32[]{:S(2)}, u32[]{:S(2)}) %collective-permute-start.53) | collective-permute-done | bytes 1568 | tf_op jit(solution)/shard_map/ppermute | solution.py:19
  289.8 4.0 %reshape.696 = f32[8,16,128]{2,1,0:T(8,128)S(1)} reshape(f32[4,2,8,2,64,2]{5,4,3,2,1,0:T(8,128)} %broadcast_in_dim.33) | data formatting | bytes 131072 | tf_op jit(solution)/shard_map/reshape | solution.py:75
  297.1 4.2 %collective-permute-done.57 = f32[1,16,128]{2,1,0:T(8,128)S(1)} collective-permute-done((f32[1,16,128]{2,1,0:T(8,128)S(1)}, f32[1,16,128]{2,1,0:T(8,128)S(1)}, u32[]{:S(2)}, u32[]{:S(2)}) %collective-permute-start.57) | collective-permute-done | bytes 8224 | tf_op jit(solution)/shard_map/ppermute | solution.py:19
  305.4 4.2 %collective-permute-done.59 = f32[10,1,128]{2,1,0:T(1,128)S(1)} collective-permute-done((f32[10,1,128]{2,1,0:T(1,128)S(1)}, f32[10,1,128]{2,1,0:T(1,128)S(1)}, u32[]{:S(2)}, u32[]{:S(2)}) %collective-permute-start.59) | collective-permute-done | bytes 5152 | tf_op jit(solution)/shard_map/ppermute | solution.py:19
  (282 shorter events, 152.0 us)
Async XLA Ops:
  0.7 30.9 %collective-permute-start = (f32[1,16,128]{2,1,0:T(8,128)S(1)}, f32[1,16,128]{2,1,0:T(8,128)S(1)}, u32[]{:S(2)}, u32[]{:S(2)}) collective-permute-start(f32[1,16,128]{2,1,0:T(8,128)S(1)} %slice.587), channel_id=1, source_target_pairs={{8,0},{16,8},{24,16},{9,1},{17,9},{25,17},{10,2},{18,10},{26,18},{... | collective-permute-start | bytes 24584 | tf_op jit(solution)/shard_map/ppermute | solution.py:27
  2.0 29.6 %collective-permute-start.2 = (f32[8,16,1]{2,1,0:T(8,128)}, f32[8,16,1]{2,1,0:T(8,128)S(1)}, u32[]{:S(2)}, u32[]{:S(2)}) collective-permute-start(f32[8,16,1]{2,1,0:T(8,128)} %bitcast.313), channel_id=1, source_target_pairs={{1,0},{3,2},{5,4},{7,6},{9,8},{11,10},{13,12},{15,14},{17,16},{19,... | collective-permute-start | bytes 1544 | tf_op jit(solution)/shard_map/ppermute | solution.py:27
  4.1 27.6 %collective-permute-start.1 = (f32[8,1,128]{2,1,0:T(1,128)S(1)}, f32[8,1,128]{2,1,0:T(1,128)S(1)}, u32[]{:S(2)}, u32[]{:S(2)}) collective-permute-start(f32[8,1,128]{2,1,0:T(1,128)S(1)} %slice.589), channel_id=1, source_target_pairs={{2,0},{4,2},{6,4},{3,1},{5,3},{7,5},{10,8},{12,10},{14,12},{11,9},... | collective-permute-start | bytes 12296 | tf_op jit(solution)/shard_map/ppermute | solution.py:27
  31.8 7.6 %collective-permute-start.3 = (f32[1,16,128]{2,1,0:T(8,128)S(1)}, f32[1,16,128]{2,1,0:T(8,128)S(1)}, u32[]{:S(2)}, u32[]{:S(2)}) collective-permute-start(f32[1,16,128]{2,1,0:T(8,128)S(1)} %get-tuple-element.49), channel_id=1, source_target_pairs={{0,8},{8,16},{16,24},{1,9},{9,17},{17,25},{2,10},{10,18},{18,26},{... | collective-permute-start | bytes 24584 | tf_op jit(solution)/shard_map/ppermute | solution.py:16
  37.4 5.5 %collective-permute-start.4 = (f32[1,16,128]{2,1,0:T(8,128)S(1)}, f32[1,16,128]{2,1,0:T(8,128)S(1)}, u32[]{:S(2)}, u32[]{:S(2)}) collective-permute-start(f32[1,16,128]{2,1,0:T(8,128)S(1)} %get-tuple-element.50), channel_id=1, source_target_pairs={{8,0},{16,8},{24,16},{9,1},{17,9},{25,17},{10,2},{18,10},{26,18},{... | collective-permute-start | bytes 24584 | tf_op jit(solution)/shard_map/ppermute | solution.py:19
  43.0 6.6 %collective-permute-start.5 = (f32[10,1,128]{2,1,0:T(1,128)S(1)}, f32[10,1,128]{2,1,0:T(1,128)S(1)}, u32[]{:S(2)}, u32[]{:S(2)}) collective-permute-start(f32[10,1,128]{2,1,0:T(1,128)S(1)} %get-tuple-element.42), channel_id=1, source_target_pairs={{0,2},{2,4},{4,6},{1,3},{3,5},{5,7},{8,10},{10,12},{12,14},{9,11},... | collective-permute-start | bytes 15368 | tf_op jit(solution)/shard_map/ppermute | solution.py:16
  47.5 6.3 %collective-permute-start.6 = (f32[10,1,128]{2,1,0:T(1,128)S(1)}, f32[10,1,128]{2,1,0:T(1,128)S(1)}, u32[]{:S(2)}, u32[]{:S(2)}) collective-permute-start(f32[10,1,128]{2,1,0:T(1,128)S(1)} %get-tuple-element.43), channel_id=1, source_target_pairs={{2,0},{4,2},{6,4},{3,1},{5,3},{7,5},{10,8},{12,10},{14,12},{11,9},... | collective-permute-start | bytes 15368 | tf_op jit(solution)/shard_map/ppermute | solution.py:19
  58.7 6.6 %collective-permute-start.10 = (f32[1,16,128]{2,1,0:T(8,128)S(1)}, f32[1,16,128]{2,1,0:T(8,128)S(1)}, u32[]{:S(2)}, u32[]{:S(2)}) collective-permute-start(f32[1,16,128]{2,1,0:T(8,128)S(1)} %get-tuple-element.48), channel_id=1, source_target_pairs={{8,0},{16,8},{24,16},{9,1},{17,9},{25,17},{10,2},{18,10},{26,18},{... | collective-permute-start | bytes 24584 | tf_op jit(solution)/shard_map/ppermute | solution.py:19
  60.0 5.9 %collective-permute-start.9 = (f32[1,16,128]{2,1,0:T(8,128)S(1)}, f32[1,16,128]{2,1,0:T(8,128)S(1)}, u32[]{:S(2)}, u32[]{:S(2)}) collective-permute-start(f32[1,16,128]{2,1,0:T(8,128)S(1)} %get-tuple-element.47), channel_id=1, source_target_pairs={{0,8},{8,16},{16,24},{1,9},{9,17},{17,25},{2,10},{10,18},{18,26},{... | collective-permute-start | bytes 24584 | tf_op jit(solution)/shard_map/ppermute | solution.py:16
  65.9 6.1 %collective-permute-start.11 = (f32[10,1,128]{2,1,0:T(1,128)S(1)}, f32[10,1,128]{2,1,0:T(1,128)S(1)}, u32[]{:S(2)}, u32[]{:S(2)}) collective-permute-start(f32[10,1,128]{2,1,0:T(1,128)S(1)} %get-tuple-element.40), channel_id=1, source_target_pairs={{0,2},{2,4},{4,6},{1,3},{3,5},{5,7},{8,10},{10,12},{12,14},{9,11},... | collective-permute-start | bytes 15368 | tf_op jit(solution)/shard_map/ppermute | solution.py:16
  70.7 5.5 %collective-permute-start.12 = (f32[10,1,128]{2,1,0:T(1,128)S(1)}, f32[10,1,128]{2,1,0:T(1,128)S(1)}, u32[]{:S(2)}, u32[]{:S(2)}) collective-permute-start(f32[10,1,128]{2,1,0:T(1,128)S(1)} %get-tuple-element.41), channel_id=1, source_target_pairs={{2,0},{4,2},{6,4},{3,1},{5,3},{7,5},{10,8},{12,10},{14,12},{11,9},... | collective-permute-start | bytes 15368 | tf_op jit(solution)/shard_map/ppermute | solution.py:19
  76.3 28.7 %collective-permute-start.13 = (f32[10,18,1]{2,1,0:T(8,128)S(1)}, f32[10,18,1]{2,1,0:T(8,128)S(1)}, u32[]{:S(2)}, u32[]{:S(2)}) collective-permute-start(f32[10,18,1]{2,1,0:T(8,128)S(1)} %get-tuple-element.34), channel_id=1, source_target_pairs={{0,1},{2,3},{4,5},{6,7},{8,9},{10,11},{12,13},{14,15},{16,17},{18,... | collective-permute-start | bytes 2168 | tf_op jit(solution)/shard_map/ppermute | solution.py:16
  77.6 27.4 %collective-permute-start.14 = (f32[10,18,1]{2,1,0:T(8,128)S(1)}, f32[10,18,1]{2,1,0:T(8,128)S(1)}, u32[]{:S(2)}, u32[]{:S(2)}) collective-permute-start(f32[10,18,1]{2,1,0:T(8,128)S(1)} %get-tuple-element.35), channel_id=1, source_target_pairs={{1,0},{3,2},{5,4},{7,6},{9,8},{11,10},{13,12},{15,14},{17,16},{19,... | collective-permute-start | bytes 2168 | tf_op jit(solution)/shard_map/ppermute | solution.py:19
  113.3 5.7 %collective-permute-start.15 = (f32[1,8,64]{2,1,0:T(8,128)S(1)}, f32[1,8,64]{2,1,0:T(8,128)S(1)}, u32[]{:S(2)}, u32[]{:S(2)}) collective-permute-start(f32[1,8,64]{2,1,0:T(8,128)S(1)} %get-tuple-element.73), channel_id=1, source_target_pairs={{0,8},{8,16},{16,24},{1,9},{9,17},{17,25},{2,10},{10,18},{18,26},{... | collective-permute-start | bytes 6152 | tf_op jit(solution)/shard_map/ppermute | solution.py:16
  117.5 5.5 %collective-permute-start.16 = (f32[1,8,64]{2,1,0:T(8,128)S(1)}, f32[1,8,64]{2,1,0:T(8,128)S(1)}, u32[]{:S(2)}, u32[]{:S(2)}) collective-permute-start(f32[1,8,64]{2,1,0:T(8,128)S(1)} %get-tuple-element.74), channel_id=1, source_target_pairs={{8,0},{16,8},{24,16},{9,1},{17,9},{25,17},{10,2},{18,10},{26,18},{... | collective-permute-start | bytes 6152 | tf_op jit(solution)/shard_map/ppermute | solution.py:19
  125.8 5.5 %collective-permute-start.18 = (f32[6,1,64]{2,1,0:T(1,128)S(1)}, f32[6,1,64]{2,1,0:T(1,128)S(1)}, u32[]{:S(2)}, u32[]{:S(2)}) collective-permute-start(f32[6,1,64]{2,1,0:T(1,128)S(1)} %get-tuple-element.62), channel_id=1, source_target_pairs={{2,0},{4,2},{6,4},{3,1},{5,3},{7,5},{10,8},{12,10},{14,12},{11,9},... | collective-permute-start | bytes 4616 | tf_op jit(solution)/shard_map/ppermute | solution.py:19
  135.9 5.5 %collective-permute-start.21 = (f32[1,8,64]{2,1,0:T(8,128)S(1)}, f32[1,8,64]{2,1,0:T(8,128)S(1)}, u32[]{:S(2)}, u32[]{:S(2)}) collective-permute-start(f32[1,8,64]{2,1,0:T(8,128)S(1)} %get-tuple-element.71), channel_id=1, source_target_pairs={{0,8},{8,16},{16,24},{1,9},{9,17},{17,25},{2,10},{10,18},{18,26},{... | collective-permute-start | bytes 6152 | tf_op jit(solution)/shard_map/ppermute | solution.py:16
  139.4 5.5 %collective-permute-start.22 = (f32[1,8,64]{2,1,0:T(8,128)S(1)}, f32[1,8,64]{2,1,0:T(8,128)S(1)}, u32[]{:S(2)}, u32[]{:S(2)}) collective-permute-start(f32[1,8,64]{2,1,0:T(8,128)S(1)} %get-tuple-element.72), channel_id=1, source_target_pairs={{8,0},{16,8},{24,16},{9,1},{17,9},{25,17},{10,2},{18,10},{26,18},{... | collective-permute-start | bytes 6152 | tf_op jit(solution)/shard_map/ppermute | solution.py:19
  144.9 4.9 %collective-permute-start.23 = (f32[6,1,64]{2,1,0:T(1,128)S(1)}, f32[6,1,64]{2,1,0:T(1,128)S(1)}, u32[]{:S(2)}, u32[]{:S(2)}) collective-permute-start(f32[6,1,64]{2,1,0:T(1,128)S(1)} %get-tuple-element.59), channel_id=1, source_target_pairs={{0,2},{2,4},{4,6},{1,3},{3,5},{5,7},{8,10},{10,12},{12,14},{9,11},... | collective-permute-start | bytes 4616 | tf_op jit(solution)/shard_map/ppermute | solution.py:16
  147.7 5.5 %collective-permute-start.24 = (f32[6,1,64]{2,1,0:T(1,128)S(1)}, f32[6,1,64]{2,1,0:T(1,128)S(1)}, u32[]{:S(2)}, u32[]{:S(2)}) collective-permute-start(f32[6,1,64]{2,1,0:T(1,128)S(1)} %get-tuple-element.60), channel_id=1, source_target_pairs={{2,0},{4,2},{6,4},{3,1},{5,3},{7,5},{10,8},{12,10},{14,12},{11,9},... | collective-permute-start | bytes 4616 | tf_op jit(solution)/shard_map/ppermute | solution.py:19
  158.5 5.0 %collective-permute-start.27 = (f32[1,4,32]{2,1,0:T(4,128)S(1)}, f32[1,4,32]{2,1,0:T(4,128)S(1)}, u32[]{:S(2)}, u32[]{:S(2)}) collective-permute-start(f32[1,4,32]{2,1,0:T(4,128)S(1)} %get-tuple-element.85), channel_id=1, source_target_pairs={{0,8},{8,16},{16,24},{1,9},{9,17},{17,25},{2,10},{10,18},{18,26},{... | collective-permute-start | bytes 1544 | tf_op jit(solution)/shard_map/ppermute | solution.py:16
  162.0 5.5 %collective-permute-start.28 = (f32[1,4,32]{2,1,0:T(4,128)S(1)}, f32[1,4,32]{2,1,0:T(4,128)S(1)}, u32[]{:S(2)}, u32[]{:S(2)}) collective-permute-start(f32[1,4,32]{2,1,0:T(4,128)S(1)} %get-tuple-element.86), channel_id=1, source_target_pairs={{8,0},{16,8},{24,16},{9,1},{17,9},{25,17},{10,2},{18,10},{26,18},{... | collective-permute-start | bytes 1544 | tf_op jit(solution)/shard_map/ppermute | solution.py:19
  170.3 5.5 %collective-permute-start.30 = (f32[4,1,32]{2,1,0:T(1,128)S(1)}, f32[4,1,32]{2,1,0:T(1,128)S(1)}, u32[]{:S(2)}, u32[]{:S(2)}) collective-permute-start(f32[4,1,32]{2,1,0:T(1,128)S(1)} %get-tuple-element.80), channel_id=1, source_target_pairs={{2,0},{4,2},{6,4},{3,1},{5,3},{7,5},{10,8},{12,10},{14,12},{11,9},... | collective-permute-start | bytes 1544 | tf_op jit(solution)/shard_map/ppermute | solution.py:19
  182.3 5.5 %collective-permute-start.34 = (f32[1,4,32]{2,1,0:T(4,128)S(1)}, f32[1,4,32]{2,1,0:T(4,128)S(1)}, u32[]{:S(2)}, u32[]{:S(2)}) collective-permute-start(f32[1,4,32]{2,1,0:T(4,128)S(1)} %get-tuple-element.84), channel_id=1, source_target_pairs={{8,0},{16,8},{24,16},{9,1},{17,9},{25,17},{10,2},{18,10},{26,18},{... | collective-permute-start | bytes 1544 | tf_op jit(solution)/shard_map/ppermute | solution.py:19
  190.6 5.5 %collective-permute-start.36 = (f32[4,1,32]{2,1,0:T(1,128)S(1)}, f32[4,1,32]{2,1,0:T(1,128)S(1)}, u32[]{:S(2)}, u32[]{:S(2)}) collective-permute-start(f32[4,1,32]{2,1,0:T(1,128)S(1)} %get-tuple-element.78), channel_id=1, source_target_pairs={{2,0},{4,2},{6,4},{3,1},{5,3},{7,5},{10,8},{12,10},{14,12},{11,9},... | collective-permute-start | bytes 1544 | tf_op jit(solution)/shard_map/ppermute | solution.py:19
  214.3 6.7 %collective-permute-start.43 = (f32[16,7,1,2,16]{4,3,1,2,0:T(2,128)S(1)}, f32[16,7,1,2,16]{4,3,1,2,0:T(2,128)S(1)}, u32[]{:S(2)}, u32[]{:S(2)}) collective-permute-start(f32[16,7,1,2,16]{4,3,1,2,0:T(2,128)S(1)} %maximum_select_fusion.1), channel_id=1, source_target_pairs={{0,16},{1,17},{2,18},{3,19},{4,20},{5,21},{6,22},{7,23},{8,24},{9,... | collective-permute-start | bytes 43016 | tf_op jit(solution)/shard_map/ppermute | solution.py:107
  247.2 5.5 %collective-permute-start.45 = (f32[1,4,32]{2,1,0:T(4,128)S(1)}, f32[1,4,32]{2,1,0:T(4,128)S(1)}, u32[]{:S(2)}, u32[]{:S(2)}) collective-permute-start(f32[1,4,32]{2,1,0:T(4,128)S(1)} %get-tuple-element.82), channel_id=1, source_target_pairs={{8,0},{16,8},{24,16},{9,1},{17,9},{25,17},{10,2},{18,10},{26,18},{... | collective-permute-start | bytes 1544 | tf_op jit(solution)/shard_map/ppermute | solution.py:19
  255.5 5.5 %collective-permute-start.47 = (f32[4,1,32]{2,1,0:T(1,128)S(1)}, f32[4,1,32]{2,1,0:T(1,128)S(1)}, u32[]{:S(2)}, u32[]{:S(2)}) collective-permute-start(f32[4,1,32]{2,1,0:T(1,128)S(1)} %get-tuple-element.76), channel_id=1, source_target_pairs={{2,0},{4,2},{6,4},{3,1},{5,3},{7,5},{10,8},{12,10},{14,12},{11,9},... | collective-permute-start | bytes 1544 | tf_op jit(solution)/shard_map/ppermute | solution.py:19
  268.5 5.5 %collective-permute-start.51 = (f32[1,8,64]{2,1,0:T(8,128)S(1)}, f32[1,8,64]{2,1,0:T(8,128)S(1)}, u32[]{:S(2)}, u32[]{:S(2)}) collective-permute-start(f32[1,8,64]{2,1,0:T(8,128)S(1)} %get-tuple-element.64), channel_id=1, source_target_pairs={{8,0},{16,8},{24,16},{9,1},{17,9},{25,17},{10,2},{18,10},{26,18},{... | collective-permute-start | bytes 6152 | tf_op jit(solution)/shard_map/ppermute | solution.py:19
  277.1 5.5 %collective-permute-start.53 = (f32[6,1,64]{2,1,0:T(1,128)S(1)}, f32[6,1,64]{2,1,0:T(1,128)S(1)}, u32[]{:S(2)}, u32[]{:S(2)}) collective-permute-start(f32[6,1,64]{2,1,0:T(1,128)S(1)} %get-tuple-element.58), channel_id=1, source_target_pairs={{2,0},{4,2},{6,4},{3,1},{5,3},{7,5},{10,8},{12,10},{14,12},{11,9},... | collective-permute-start | bytes 4616 | tf_op jit(solution)/shard_map/ppermute | solution.py:19
  295.7 5.5 %collective-permute-start.57 = (f32[1,16,128]{2,1,0:T(8,128)S(1)}, f32[1,16,128]{2,1,0:T(8,128)S(1)}, u32[]{:S(2)}, u32[]{:S(2)}) collective-permute-start(f32[1,16,128]{2,1,0:T(8,128)S(1)} %get-tuple-element.45), channel_id=1, source_target_pairs={{8,0},{16,8},{24,16},{9,1},{17,9},{25,17},{10,2},{18,10},{26,18},{... | collective-permute-start | bytes 24584 | tf_op jit(solution)/shard_map/ppermute | solution.py:19
  304.1 5.5 %collective-permute-start.59 = (f32[10,1,128]{2,1,0:T(1,128)S(1)}, f32[10,1,128]{2,1,0:T(1,128)S(1)}, u32[]{:S(2)}, u32[]{:S(2)}) collective-permute-start(f32[10,1,128]{2,1,0:T(1,128)S(1)} %get-tuple-element.39), channel_id=1, source_target_pairs={{2,0},{4,2},{6,4},{3,1},{5,3},{7,5},{10,8},{12,10},{14,12},{11,9},... | collective-permute-start | bytes 15368 | tf_op jit(solution)/shard_map/ppermute | solution.py:19
  (34 other events, 130.9 us)
